TPU v7x, 256 devices: a whole 4x4x8 slice. The times are simulated.
256 devices in a mesh: narrow: 8 (over y, core), wide: 32 (over x, z).
Axes of the slice: x: 4, y: 4, z: 8, core: 2. Of those that a mesh axis runs over, the one named last changes fastest.
Arguments:
- points: float32 [2, 32768], P(None, ('narrow', 'wide')), may hold values from 0 to 1
- quad_weight: float32 [32768], P(('narrow', 'wide')), may hold values from 9.155274e-06 to 9.1552734e-05
- basis: float32 [4, 2, 32768, 128], P(None, None, ('narrow', 'wide')), may hold values from -6 to 6
- jacobi: float32 [2, 32768], P(None, ('narrow', 'wide')), may hold values from 0.5 to 2
- near_panel: int32 [2048, 12], P(('narrow', 'wide')), may hold values from 0 to 2047, as said below
- near_count: int32 [2048], P(('narrow', 'wide')), may hold values from 2 to 12, as said below
- near_block: bfloat16 [2048, 12, 32, 32], P(('narrow', 'wide')), may hold values from -0.875 to 0.875
- agg_index: int32 [2, 32768], P(None, ('narrow', 'wide')), may hold values from 0 to 47
- coarse_inverse: float32 [8, 1536, 12288], P(None, 'wide', 'narrow'), may hold values from -0.1 to 0.5
Outputs:
- new_block: float32 [2, 32768, 128], P(None, ('narrow', 'wide'))
- hessenberg: float32 [4, 128, 128], replicated
- upper_factor: float32 [128, 128], replicated
Inputs may be any that keep to these rules, and one draw needn't show every extreme that they name: near_panel[p, 0] = p; every entry lies within 4 panels of p in panel order, and some entry lies exactly 4 panels away. `near_count`: slots at or beyond a panel's count are not used; some panel uses all 12.
All inputs are finite; a program needn't handle non-finite values.
Results may differ from a plain program's by a relative error of at most 0.0027.
The roundings to bfloat16 on the way count: a program that leaves them out, or rounds other values in their place, can miss the bound.
Values may be sent and summed in bfloat16 or wider, within the bound.
A program may use at most 64 MiB of HBM per device.

v0:
```python
import math
import jax
import jax.numpy as jnp
from jax import lax
from jax.sharding import PartitionSpec as P

SPAN = 4
NU = 0.3
DELTA2 = 1e-05
ELASTIC = 40.0
HIGH = lax.Precision.HIGHEST


def extended(block, sides, width):
    for axis, dim in sides:
        count = lax.axis_size(axis)
        forward = [(i, i + 1) for i in range(count - 1)]
        backward = [(target, source) for source, target in forward]
        low = lax.ppermute(
            lax.slice_in_dim(block, block.shape[dim] - width, None, axis=dim), axis, forward
        )
        high = lax.ppermute(lax.slice_in_dim(block, 0, width, axis=dim), axis, backward)
        block = jnp.concatenate([low, block, high], axis=dim)
    return block


def far_kernel(targets, sources, weights):
    delta_x = targets[0][:, None] - sources[0][None, :]
    delta_y = targets[1][:, None] - sources[1][None, :]
    square_dist = delta_x * delta_x + delta_y * delta_y + DELTA2
    factor = ELASTIC * weights[None, :]
    log_part = -0.5 * (3.0 - 4.0 * NU) * jnp.log(square_dist)
    g_xx = factor * (log_part + delta_x * delta_x / square_dist)
    g_xy = factor * (delta_x * delta_y / square_dist)
    g_yy = factor * (log_part + delta_y * delta_y / square_dist)
    first_row = jnp.stack([g_xx, g_xy], axis=1)
    second_row = jnp.stack([g_xy, g_yy], axis=1)
    stacked = jnp.stack([first_row, second_row], axis=0)
    return stacked.reshape(2 * targets.shape[1], 2 * sources.shape[1]).astype(jnp.bfloat16)


def far_product(targets, sources, weights, fields):
    piece_len = sources.shape[1]
    row_count = targets.shape[1]
    rhs_count = fields.shape[2]
    block_size = math.gcd(piece_len, max(512, 524288 // row_count))
    block_count = piece_len // block_size

    def one_block(block_index, running):
        offset = block_index * block_size
        source_block = lax.dynamic_slice_in_dim(sources, offset, block_size, 1)
        weight_block = lax.dynamic_slice_in_dim(weights, offset, block_size, 0)
        field_block = lax.dynamic_slice_in_dim(fields, offset, block_size, 1)
        kernel_block = far_kernel(targets, source_block, weight_block)
        return running + jnp.dot(
            kernel_block,
            field_block.reshape(2 * block_size, rhs_count),
            preferred_element_type=jnp.float32,
        )

    initial = jnp.zeros((2 * row_count, rhs_count), jnp.float32)
    return lax.fori_loop(0, block_count, one_block, initial)


def make_fold(targets, source_all, shard_piece):
    return far_product(targets, source_all[0:2], source_all[2], shard_piece)


def body(
    points,
    quad_weight,
    basis,
    jacobi,
    near_panel,
    near_count,
    near_block,
    agg_index,
    coarse_inverse,
):
    block_total = basis.shape[0]
    point_count = basis.shape[2]
    rhs_count = basis.shape[3]
    coarse_count = coarse_inverse.shape[1]
    newest = basis[block_total - 1]
    member = (
        agg_index[:, :, None] == jnp.arange(coarse_count, dtype=jnp.int32)[None, None, :]
    ).astype(jnp.float32)
    coarse_rhs = jnp.einsum("apc,apr->cr", member, newest, precision=HIGH)
    coarse_part = jnp.einsum(
        "abc,cr->abr",
        coarse_inverse,
        lax.all_gather(coarse_rhs, "wide", axis=0, tiled=True),
        precision=HIGH,
    )
    coarse_sol = lax.psum_scatter(coarse_part, "narrow", scatter_dimension=0, tiled=True)[0]
    lifted = jnp.einsum("apc,cr->apr", member, coarse_sol, precision=HIGH)
    precond = (jacobi[:, :, None] * newest + lifted).astype(jnp.bfloat16)
    source_info = jnp.concatenate([points, quad_weight[None, :]], axis=0)
    targets = lax.all_gather(points, "narrow", axis=1, tiled=True)
    source_all = lax.all_gather(source_info, "wide", axis=1, tiled=True)
    far_part = make_fold(targets, source_all, lax.all_gather(precond, "wide", axis=1, tiled=True))
    far_local = lax.psum_scatter(
        far_part.reshape(2, targets.shape[1], rhs_count), "narrow", scatter_dimension=1, tiled=True
    )
    panels_dev = near_panel.shape[0]
    slot_total = near_panel.shape[1]
    nodes = near_block.shape[2] // 2
    padded = extended(precond, ((("narrow", "wide"), 1),), SPAN * nodes)
    panel_fields = padded.reshape(2, panels_dev + 2 * SPAN, nodes, rhs_count)
    local_index = near_panel - lax.axis_index(("narrow", "wide")) * panels_dev + SPAN
    gathered = panel_fields[:, local_index]
    slot_live = jnp.arange(slot_total, dtype=jnp.int32)[None, :] < near_count[:, None]
    gathered = jnp.where(slot_live[None, :, :, None, None], gathered, jnp.zeros((), gathered.dtype))
    gathered = jnp.transpose(gathered, (1, 2, 0, 3, 4)).reshape(
        panels_dev, slot_total, 2 * nodes, rhs_count
    )
    near_terms = jnp.einsum(
        "pkxy,pkyr->pxr", near_block, gathered, preferred_element_type=jnp.float32
    )
    near = jnp.transpose(near_terms.reshape(panels_dev, 2, nodes, rhs_count), (1, 0, 2, 3)).reshape(
        2, point_count, rhs_count
    )
    image = 0.5 * precond.astype(jnp.float32) + far_local + near
    weighted = basis * quad_weight[None, None, :, None]
    local_proj = jnp.einsum("jair,aiw->jrw", weighted, image, precision=HIGH)
    hessenberg = lax.psum(local_proj, ("narrow", "wide"))
    remainder = image - jnp.einsum("jair,jrw->aiw", basis, hessenberg, precision=HIGH)
    local_gram = jnp.einsum(
        "air,aiw->rw", remainder * quad_weight[None, :, None], remainder, precision=HIGH
    )
    gram_matrix = lax.psum(local_gram, ("narrow", "wide"))
    lower_factor = jnp.linalg.cholesky(gram_matrix)
    flat = remainder.reshape(2 * point_count, rhs_count)
    solved = jax.scipy.linalg.solve_triangular(lower_factor, flat.T, lower=True)
    new_block = solved.T.reshape(2, point_count, rhs_count)
    return (new_block, hessenberg, lower_factor.T)


def solution(mesh):
    in_specs = (
        P(None, ("narrow", "wide")),
        P(("narrow", "wide")),
        P(None, None, ("narrow", "wide"), None),
        P(None, ("narrow", "wide")),
        P(("narrow", "wide"), None),
        P(("narrow", "wide")),
        P(("narrow", "wide"), None, None, None),
        P(None, ("narrow", "wide")),
        P(None, "wide", "narrow"),
    )
    out_specs = (P(None, ("narrow", "wide"), None), P(), P())
    return jax.shard_map(body, mesh=mesh, in_specs=in_specs, out_specs=out_specs, check_vma=False)
```

profile of v0, /device:TPU:1, one launch (start us, length us, event | category | flops | bytes accessed | tf_op | source)
XLA Modules:
  0.0 911.1 jit_solution(4539948616988339396)
XLA Ops:
  8.5 42.3 %all_gather.12 = f32[1536,128]{1,0:T(8,128)S(1)} all-gather(f32[48,128]{1,0:T(8,128)S(1)} %convolution_bitcast_fusion.4), channel_id=1, replica_groups=mesh['narrow'=8,'wide'=32] {'wide'}, dimensions={0}, use_global_device_ids=true | all-gather | bytes 811008 | tf_op jit(solution)/shard_map/all_gather | solution.py:92
  53.6 40.3 %reduce-scatter.3.cloned.1.call-done = f32[1,48,128]{2,1,0:T(8,128)} async-done(((f32[8,48,128]{2,1,0:T(8,128)}), f32[1,48,128]{2,1,0:T(8,128)}) %reduce-scatter.3.cloned.1.call-update) | async-done | bytes 24592 | tf_op jit(solution)/shard_map/reduce_scatter | solution.py:95
  95.9 38.2 %all_gather.13 = f32[3,4096]{1,0:T(4,128)S(1)} all-gather(f32[3,128]{1,0:T(4,128)S(1)} %pad_maximum_fusion.2), channel_id=1, replica_groups=mesh['narrow'=8,'wide'=32] {'wide'}, dimensions={1}, use_global_device_ids=true | all-gather | bytes 50688 | tf_op jit(solution)/shard_map/all_gather | solution.py:100
  134.2 22.4 %all_gather.14 = f32[2,1024]{1,0:T(2,128)S(1)} all-gather(f32[2,128]{1,0:T(2,128)S(1)} %copy-done.8), channel_id=1, replica_groups=mesh['narrow'=8,'wide'=32] {'narrow'}, dimensions={1}, use_global_device_ids=true | all-gather | bytes 9216 | tf_op jit(solution)/shard_map/all_gather | solution.py:99
  156.6 14.8 %all-gather.2.cloned.1.call-done = bf16[2,4096,128]{2,1,0:T(8,128)(2,1)} async-done(((bf16[2,128,128]{2,1,0:T(8,128)(2,1)}), bf16[2,4096,128]{2,1,0:T(8,128)(2,1)}) %all-gather.2.cloned.1.call-update) | async-done | bytes 2097168 | tf_op jit(solution)/shard_map/all_gather | solution.py:101
  171.5 163.6 %while.14 = (s32[]{:T(128)}, f32[2048,128]{1,0:T(8,128)}, f32[4096]{0:T(1024)S(1)}, f32[2,1024]{1,0:T(2,128)S(1)}, f32[2,4096]{1,0:T(2,128)S(1)}, /*index=5*/bf1...) while((s32[]{:T(128)}, f32[2048,128]{1,0:T(8,128)}, ...), condition=%wide.region_2.0_spmd.clone, body=%wide.region_1.0_spmd.clone.sunk | while | flops 551551488 | bytes 51161332 | solution.py:62
  174.0 6.3 copy.58
  180.3 5.4 copy.59
  194.4 6.3 copy.58
  200.7 5.4 copy.59
  214.9 6.3 copy.58
  235.3 6.3 copy.58
  255.8 6.3 copy.58
  276.2 6.3 copy.58
  282.5 5.4 copy.59
  296.7 6.3 copy.58
  303.0 5.4 copy.59
  317.1 6.3 copy.58
  337.7 8.7 collective-permute-start.1
  352.0 17.6 %reduce-scatter.5.cloned.1.call-done = f32[2,128,128]{2,1,0:T(8,128)} async-done(((f32[2,1024,128]{2,1,0:T(8,128)}), f32[2,128,128]{2,1,0:T(8,128)}) %reduce-scatter.5.cloned.1.call-update) | async-done | bytes 131088 | tf_op jit(solution)/shard_map/reduce_scatter | solution.py:102
  372.6 256.9 %all-reduce.3.cloned.1.call-done = f32[4,128,128]{2,1,0:T(8,128)} async-done(((f32[4,128,128]{2,1,0:T(8,128)}), f32[4,128,128]{2,1,0:T(8,128)}) %all-reduce.3.cloned.1.call-update) | async-done | bytes 262160 | tf_op jit(solution)/shard_map/psum | solution.py:126
  632.2 245.4 %all-reduce.5.cloned.1.call-done = f32[128,128]{0,1:T(8,128)} async-done(((f32[128,128]{0,1:T(8,128)}), f32[128,128]{0,1:T(8,128)}) %all-reduce.5.cloned.1.call-update) | async-done | bytes 65552 | tf_op jit(solution)/shard_map/psum | solution.py:131
  879.4 11.7 %cholesky.16 = f32[128,128]{1,0:T(8,128)S(1)} custom-call(f32[128,128]{1,0:T(8,128)S(1)} %fusion.27), custom_call_target="Cholesky" | custom-call | tf_op jit(solution)/shard_map/jit(cholesky)/cholesky | solution.py:132
  892.4 9.8 %custom-call.7 = f32[1,128,128]{1,2,0:T(8,128)S(1)} custom-call(f32[1,128,128]{2,1,0:T(8,128)S(1)} %get-tuple-element.165), custom_call_target="InvertDiagBlocksLowerTriangular" | custom-call | tf_op jit(solution)/shard_map/jit(_solve_triangular)/triangular_solve | solution.py:134
  (162 shorter events, 116.5 us)
Async XLA Ops:
  7.2 43.7 %copy-start = (f32[8,48,1536]{2,1,0:T(8,128)S(1)}, f32[8,48,1536]{2,1,0:T(8,128)}, u32[]{:S(2)}) copy-start(f32[8,48,1536]{2,1,0:T(8,128)} %param.19) | copy-start | bytes 7077892
  7.2 86.8 %reduce-scatter.3.cloned.1.call-start = ((), (), s32[]{:S(2)}) async-start(), calls=%async_computation.2 | async-start | bytes 221184 | tf_op jit(solution)/shard_map/reduce_scatter | solution.py:95
  8.5 85.5 %copy-start.7 = (s32[2,128]{1,0:T(2,128)S(1)}, s32[2,128]{1,0:T(2,128)}, u32[]{:S(2)}) copy-start(s32[2,128]{1,0:T(2,128)} %param.18) | copy-start | bytes 3076
  8.5 85.5 %copy-start.10 = (f32[2,128]{1,0:T(2,128)S(1)}, f32[2,128]{1,0:T(2,128)}, u32[]{:S(2)}) copy-start(f32[2,128]{1,0:T(2,128)} %param.14) | copy-start | bytes 3076
  50.9 45.1 %copy-start.6 = (f32[128]{0:T(128)S(1)}, f32[128]{0:T(128)}, u32[]{:S(2)}) copy-start(f32[128]{0:T(128)} %param.12) | copy-start | bytes 1540
  50.9 45.1 %copy-start.8 = (f32[2,128]{1,0:T(2,128)S(1)}, f32[2,128]{1,0:T(2,128)}, u32[]{:S(2)}) copy-start(f32[2,128]{1,0:T(2,128)} %param.11) | copy-start | bytes 3076
  53.6 117.9 %all-gather.2.cloned.1.call-start = ((), (), s32[]{:S(2)}) async-start(), calls=%async_computation.3 | async-start | bytes 2162688 | tf_op jit(solution)/shard_map/all_gather | solution.py:101
  95.9 273.8 %reduce-scatter.5.cloned.1.call-start = ((), (), s32[]{:S(2)}) async-start(), calls=%async_computation.4 | async-start | bytes 1179648 | tf_op jit(solution)/shard_map/reduce_scatter | solution.py:102
  171.5 163.7 %copy-start.9 = (s32[8,12]{1,0:T(8,128)S(1)}, s32[8,12]{1,0:T(8,128)}, u32[]{:S(2)}) copy-start(s32[8,12]{1,0:T(8,128)} %param.15) | copy-start | bytes 1156
  171.5 163.8 %copy-start.11 = (s32[8]{0:T(128)S(1)}, s32[8]{0:T(128)}, u32[]{:S(2)}) copy-start(s32[8]{0:T(128)} %param.16) | copy-start | bytes 100
  171.5 163.8 %copy-start.4 = (bf16[2,128,128]{2,1,0:T(8,128)(2,1)S(1)}, bf16[2,128,128]{2,1,0:T(8,128)(2,1)}, u32[]{:S(2)}) copy-start(bf16[2,128,128]{2,1,0:T(8,128)(2,1)} %fusion.16) | copy-start | bytes 196612
  180.3 7.1 copy-start.1
  200.7 7.1 copy-start.1
  221.2 7.1 copy-start.1
  241.6 7.1 copy-start.1
  262.1 7.1 copy-start.1
  282.5 7.1 copy-start.1
  303.0 7.1 copy-start.1
  335.1 294.4 %all-reduce.3.cloned.1.call-start = ((), (), s32[]{:S(2)}) async-start(), calls=%async_computation.5 | async-start | bytes 524288 | tf_op jit(solution)/shard_map/psum | solution.py:126
  335.3 11.1 %collective-permute-start = (bf16[2,64,128]{2,1,0:T(8,128)(2,1)S(1)}, bf16[2,64,128]{2,1,0:T(8,128)(2,1)S(1)}, u32[]{:S(2)}, u32[]{:S(2)}) collective-permute-start(bf16[2,64,128]{2,1,0:T(8,128)(2,1)S(1)} %get-tuple-element.166), channel_id=1, source_target_pairs={{0,1},{1,2},{2,3},{3,4},{4,5},{5,6},{6,7},{7,8},{8,9},{9,10},{10,1... | collective-permute-start | bytes 98312 | tf_op jit(solution)/shard_map/ppermute | solution.py:19
  337.7 9.7 %collective-permute-start.1 = (bf16[2,64,128]{2,1,0:T(8,128)(2,1)S(1)}, bf16[2,64,128]{2,1,0:T(8,128)(2,1)S(1)}, u32[]{:S(2)}, u32[]{:S(2)}) collective-permute-start(bf16[2,64,128]{2,1,0:T(8,128)(2,1)S(1)} %get-tuple-element.167), channel_id=1, source_target_pairs={{1,0},{2,1},{3,2},{4,3},{5,4},{6,5},{7,6},{8,7},{9,8},{10,9},{11,1... | collective-permute-start | bytes 98312 | tf_op jit(solution)/shard_map/ppermute | solution.py:22
  349.0 21.5 %copy-start.3 = (f32[4,2,128,128]{3,2,1,0:T(8,128)S(1)}, f32[4,2,128,128]{3,2,1,0:T(8,128)}, u32[]{:S(2)}) copy-start(f32[4,2,128,128]{3,2,1,0:T(8,128)} %param.13) | copy-start | bytes 1572868
  372.4 505.2 %all-reduce.5.cloned.1.call-start = ((), (), s32[]{:S(2)}) async-start(), calls=%async_computation.6 | async-start | bytes 131072 | tf_op jit(solution)/shard_map/psum | solution.py:131
  629.5 274.4 %copy-start.5 = (f32[4,128,128]{2,1,0:T(8,128)S(1)}, f32[4,128,128]{2,1,0:T(8,128)}, u32[]{:S(2)}) copy-start(f32[4,128,128]{2,1,0:T(8,128)} %all-reduce.3.cloned.1.call-done) | copy-start | bytes 786436
  (9 other events, 14.9 us)
Sparse Core Ops, SparseCore 0:
  53.7 40.2 reduce-scatter.2
  97.1 74.2 all-gather.1
  335.2 34.3 reduce-scatter.4
  375.5 253.9 all-reduce.2
  635.4 242.0 all-reduce.4
where the time goes:
time: 912 us; the launch traced here: 911 us
  waiting for transfers between devices  576 us (63%)
  local copies, waits for them, and re-layouts  120 us (13%)
  blocking collectives  103 us (11%)
  other arithmetic  45.4 us (5%)
  matrix products  41.1 us (5%)
  between operations  14 us (2%)
  starting transfers between devices  11.5 us (1%)
    psum x1, waiting for transfers between devices, body(): hessenberg = lax.psum(local_proj, ('narrow', 'wide'))  257 us
    psum x1, waiting for transfers between devices, body(): gram_matrix = lax.psum(local_gram, ('narrow', 'wide'))  245 us
    while x40, local copies, waits for them, and re-layouts  51.2 us
    another operation x8, local copies, waits for them, and re-layouts, far_kernel(): stacked = jnp.stack([first_row, second_row], axis=0)  50.4 us
    all_gather x1, blocking collectives, body(): lax.all_gather(coarse_rhs, 'wide', axis=0, tiled=True)  42.3 us
    reduce_scatter x1, waiting for transfers between devices, body(): lax.psum_scatter(coarse_part, 'narrow', scatter_dimension=0, tiled=True)[0]  40.3 us
    all_gather x1, blocking collectives, body(): source_all = lax.all_gather(source_info, 'wide', axis=1, tiled=True)  38.2 us
    dot_general x8, matrix products, one_block(): jnp.dot(kernel_block, field_block.reshape(2 * block_size, rhs_count), pre...  28.3 us
  transfers between devices with their start and end apart: 7, of which 6 were waited for; matrix products, arithmetic and copies ran while one was open for 1% of the time, Pallas kernels for 0%

commit v1 on v0

--- a/solution.py
+++ b/solution.py
@@ -123,7 +123,7 @@
     image = 0.5 * precond.astype(jnp.float32) + far_local + near
     weighted = basis * quad_weight[None, None, :, None]
     local_proj = jnp.einsum("jair,aiw->jrw", weighted, image, precision=HIGH)
-    hessenberg = lax.psum(local_proj, ("narrow", "wide"))
+    hessenberg = lax.psum(lax.psum(local_proj, "narrow"), "wide")
     remainder = image - jnp.einsum("jair,jrw->aiw", basis, hessenberg, precision=HIGH)
     local_gram = jnp.einsum(
         "air,aiw->rw", remainder * quad_weight[None, :, None], remainder, precision=HIGH

time: 912 us -> 866 us (0.950)
  waiting for transfers between devices: 576 us -> 530 us
    psum x1 -> x2, waiting for transfers between devices: 257 us -> 210 us  [body(): hessenberg = lax.psum(lax.psum(local_proj, 'narrow'), 'wide')]
  transfers between devices with their start and end apart: 7 -> 8, of which waited for: 6 -> 7; matrix products, arithmetic and copies ran while one was open for 1% -> 1% of each run, Pallas kernels for 0% -> 0%
where the time goes in v1:
time: 866 us
  waiting for transfers between devices  530 us (61%)
  local copies, waits for them, and re-layouts  120 us (14%)
  blocking collectives  103 us (12%)
  other arithmetic  45.4 us (5%)
  matrix products  41.1 us (5%)
  between operations  14.3 us (2%)
  starting transfers between devices  11.5 us (1%)
    psum x1, waiting for transfers between devices, body(): gram_matrix = lax.psum(local_gram, ('narrow', 'wide'))  246 us
    psum x2, waiting for transfers between devices, body(): hessenberg = lax.psum(lax.psum(local_proj, 'narrow'), 'wide')  210 us
    while x40, local copies, waits for them, and re-layouts  51.2 us
    another operation x8, local copies, waits for them, and re-layouts, far_kernel(): stacked = jnp.stack([first_row, second_row], axis=0)  50.4 us
    all_gather x1, blocking collectives, body(): lax.all_gather(coarse_rhs, 'wide', axis=0, tiled=True)  42.3 us
    reduce_scatter x1, waiting for transfers between devices, body(): lax.psum_scatter(coarse_part, 'narrow', scatter_dimension=0, tiled=True)[0]  40.3 us
    all_gather x1, blocking collectives, body(): source_all = lax.all_gather(source_info, 'wide', axis=1, tiled=True)  38.2 us
    dot_general x8, matrix products, one_block(): jnp.dot(kernel_block, field_block.reshape(2 * block_size, rhs_count), pre...  28.3 us
  transfers between devices with their start and end apart: 8, of which 7 were waited for; matrix products, arithmetic and copies ran while one was open for 1% of the time, Pallas kernels for 0%

profile of v1, /device:TPU:1, one launch (start us, length us, event | category | flops | bytes accessed | tf_op | source)
XLA Modules:
  0.0 865.8 jit_solution(13826240138039921814)
XLA Ops:
  8.5 42.3 %all_gather.12 = f32[1536,128]{1,0:T(8,128)S(1)} all-gather(f32[48,128]{1,0:T(8,128)S(1)} %convolution_bitcast_fusion.4), channel_id=1, replica_groups=mesh['narrow'=8,'wide'=32] {'wide'}, dimensions={0}, use_global_device_ids=true | all-gather | bytes 811008 | tf_op jit(solution)/shard_map/all_gather | solution.py:92
  53.6 40.3 %reduce-scatter.3.cloned.1.call-done = f32[1,48,128]{2,1,0:T(8,128)} async-done(((f32[8,48,128]{2,1,0:T(8,128)}), f32[1,48,128]{2,1,0:T(8,128)}) %reduce-scatter.3.cloned.1.call-update) | async-done | bytes 24592 | tf_op jit(solution)/shard_map/reduce_scatter | solution.py:95
  95.9 38.2 %all_gather.13 = f32[3,4096]{1,0:T(4,128)S(1)} all-gather(f32[3,128]{1,0:T(4,128)S(1)} %pad_maximum_fusion.2), channel_id=1, replica_groups=mesh['narrow'=8,'wide'=32] {'wide'}, dimensions={1}, use_global_device_ids=true | all-gather | bytes 50688 | tf_op jit(solution)/shard_map/all_gather | solution.py:100
  134.2 22.4 %all_gather.14 = f32[2,1024]{1,0:T(2,128)S(1)} all-gather(f32[2,128]{1,0:T(2,128)S(1)} %copy-done.8), channel_id=1, replica_groups=mesh['narrow'=8,'wide'=32] {'narrow'}, dimensions={1}, use_global_device_ids=true | all-gather | bytes 9216 | tf_op jit(solution)/shard_map/all_gather | solution.py:99
  156.6 14.8 %all-gather.2.cloned.1.call-done = bf16[2,4096,128]{2,1,0:T(8,128)(2,1)} async-done(((bf16[2,128,128]{2,1,0:T(8,128)(2,1)}), bf16[2,4096,128]{2,1,0:T(8,128)(2,1)}) %all-gather.2.cloned.1.call-update) | async-done | bytes 2097168 | tf_op jit(solution)/shard_map/all_gather | solution.py:101
  171.5 163.6 %while.14 = (s32[]{:T(128)}, f32[2048,128]{1,0:T(8,128)}, f32[4096]{0:T(1024)S(1)}, f32[2,1024]{1,0:T(2,128)S(1)}, f32[2,4096]{1,0:T(2,128)S(1)}, /*index=5*/bf1...) while((s32[]{:T(128)}, f32[2048,128]{1,0:T(8,128)}, ...), condition=%wide.region_2.0_spmd.clone, body=%wide.region_1.0_spmd.clone.sunk | while | flops 551551488 | bytes 51161332 | solution.py:62
  174.0 6.3 copy.58
  180.3 5.4 copy.59
  194.4 6.3 copy.58
  200.7 5.4 copy.59
  214.9 6.3 copy.58
  235.3 6.3 copy.58
  255.8 6.3 copy.58
  276.2 6.3 copy.58
  282.5 5.4 copy.59
  296.7 6.3 copy.58
  317.1 6.3 copy.58
  337.7 8.7 %collective-permute-start.1 = (bf16[2,64,128]{2,1,0:T(8,128)(2,1)S(1)}, bf16[2,64,128]{2,1,0:T(8,128)(2,1)S(1)}, u32[]{:S(2)}, u32[]{:S(2)}) collective-permute-start(bf16[2,64,128]{2,1,0:T(8,128)(2,1)S(1)} %get-tuple-element.167), channel_id=1, source_target_pairs={{1,0},{2,1},{3,2},{4,3},{5,4},{6,5},{7,6},{8,7},{9,8},{10,9},{11,1... | collective-permute-start | bytes 98312 | tf_op jit(solution)/shard_map/ppermute | solution.py:22
  352.0 17.6 %reduce-scatter.5.cloned.1.call-done = f32[2,128,128]{2,1,0:T(8,128)} async-done(((f32[2,1024,128]{2,1,0:T(8,128)}), f32[2,128,128]{2,1,0:T(8,128)}) %reduce-scatter.5.cloned.1.call-update) | async-done | bytes 131088 | tf_op jit(solution)/shard_map/reduce_scatter | solution.py:102
  372.4 64.7 %all-reduce.4.cloned.1.call-done = f32[4,128,128]{2,1,0:T(8,128)} async-done(((f32[4,128,128]{2,1,0:T(8,128)}), f32[4,128,128]{2,1,0:T(8,128)}) %all-reduce.4.cloned.1.call-update) | async-done | bytes 262160 | tf_op jit(solution)/shard_map/psum | solution.py:126
  437.4 145.4 %all-reduce.6.cloned.1.call-done = f32[4,128,128]{2,1,0:T(8,128)} async-done(((f32[4,128,128]{2,1,0:T(8,128)}), f32[4,128,128]{2,1,0:T(8,128)}) %all-reduce.6.cloned.1.call-update) | async-done | bytes 262160 | tf_op jit(solution)/shard_map/psum | solution.py:126
  585.5 246.5 %all-reduce.8.cloned.1.call-done = f32[128,128]{0,1:T(8,128)} async-done(((f32[128,128]{0,1:T(8,128)}), f32[128,128]{0,1:T(8,128)}) %all-reduce.8.cloned.1.call-update) | async-done | bytes 65552 | tf_op jit(solution)/shard_map/psum | solution.py:131
  833.7 11.7 %cholesky.16 = f32[128,128]{1,0:T(8,128)S(1)} custom-call(f32[128,128]{1,0:T(8,128)S(1)} %fusion.27), custom_call_target="Cholesky" | custom-call | tf_op jit(solution)/shard_map/jit(cholesky)/cholesky | solution.py:132
  846.8 9.8 %custom-call.7 = f32[1,128,128]{1,2,0:T(8,128)S(1)} custom-call(f32[1,128,128]{2,1,0:T(8,128)S(1)} %get-tuple-element.165), custom_call_target="InvertDiagBlocksLowerTriangular" | custom-call | tf_op jit(solution)/shard_map/jit(_solve_triangular)/triangular_solve | solution.py:134
  (165 shorter events, 121.9 us)
Async XLA Ops:
  7.2 43.7 %copy-start = (f32[8,48,1536]{2,1,0:T(8,128)S(1)}, f32[8,48,1536]{2,1,0:T(8,128)}, u32[]{:S(2)}) copy-start(f32[8,48,1536]{2,1,0:T(8,128)} %param.19) | copy-start | bytes 7077892
  7.2 86.8 %reduce-scatter.3.cloned.1.call-start = ((), (), s32[]{:S(2)}) async-start(), calls=%async_computation.2 | async-start | bytes 221184 | tf_op jit(solution)/shard_map/reduce_scatter | solution.py:95
  8.5 85.5 %copy-start.7 = (s32[2,128]{1,0:T(2,128)S(1)}, s32[2,128]{1,0:T(2,128)}, u32[]{:S(2)}) copy-start(s32[2,128]{1,0:T(2,128)} %param.18) | copy-start | bytes 3076
  8.5 85.5 %copy-start.10 = (f32[2,128]{1,0:T(2,128)S(1)}, f32[2,128]{1,0:T(2,128)}, u32[]{:S(2)}) copy-start(f32[2,128]{1,0:T(2,128)} %param.14) | copy-start | bytes 3076
  50.9 45.1 %copy-start.6 = (f32[128]{0:T(128)S(1)}, f32[128]{0:T(128)}, u32[]{:S(2)}) copy-start(f32[128]{0:T(128)} %param.12) | copy-start | bytes 1540
  50.9 45.1 %copy-start.8 = (f32[2,128]{1,0:T(2,128)S(1)}, f32[2,128]{1,0:T(2,128)}, u32[]{:S(2)}) copy-start(f32[2,128]{1,0:T(2,128)} %param.11) | copy-start | bytes 3076
  53.6 117.9 %all-gather.2.cloned.1.call-start = ((), (), s32[]{:S(2)}) async-start(), calls=%async_computation.3 | async-start | bytes 2162688 | tf_op jit(solution)/shard_map/all_gather | solution.py:101
  95.9 273.8 %reduce-scatter.5.cloned.1.call-start = ((), (), s32[]{:S(2)}) async-start(), calls=%async_computation.4 | async-start | bytes 1179648 | tf_op jit(solution)/shard_map/reduce_scatter | solution.py:102
  171.5 163.7 %copy-start.9 = (s32[8,12]{1,0:T(8,128)S(1)}, s32[8,12]{1,0:T(8,128)}, u32[]{:S(2)}) copy-start(s32[8,12]{1,0:T(8,128)} %param.15) | copy-start | bytes 1156
  171.5 163.8 %copy-start.11 = (s32[8]{0:T(128)S(1)}, s32[8]{0:T(128)}, u32[]{:S(2)}) copy-start(s32[8]{0:T(128)} %param.16) | copy-start | bytes 100
  171.5 163.8 %copy-start.4 = (bf16[2,128,128]{2,1,0:T(8,128)(2,1)S(1)}, bf16[2,128,128]{2,1,0:T(8,128)(2,1)}, u32[]{:S(2)}) copy-start(bf16[2,128,128]{2,1,0:T(8,128)(2,1)} %fusion.16) | copy-start | bytes 196612
  180.3 7.1 copy-start.1
  200.7 7.1 copy-start.1
  221.2 7.1 copy-start.1
  241.6 7.1 copy-start.1
  262.1 7.1 copy-start.1
  282.5 7.1 copy-start.1
  335.1 102.0 %all-reduce.4.cloned.1.call-start = ((), (), s32[]{:S(2)}) async-start(), calls=%async_computation.5 | async-start | bytes 524288 | tf_op jit(solution)/shard_map/psum | solution.py:126
  335.3 11.1 %collective-permute-start = (bf16[2,64,128]{2,1,0:T(8,128)(2,1)S(1)}, bf16[2,64,128]{2,1,0:T(8,128)(2,1)S(1)}, u32[]{:S(2)}, u32[]{:S(2)}) collective-permute-start(bf16[2,64,128]{2,1,0:T(8,128)(2,1)S(1)} %get-tuple-element.166), channel_id=1, source_target_pairs={{0,1},{1,2},{2,3},{3,4},{4,5},{5,6},{6,7},{7,8},{8,9},{9,10},{10,1... | collective-permute-start | bytes 98312 | tf_op jit(solution)/shard_map/ppermute | solution.py:19
  337.7 9.7 %collective-permute-start.1 = (bf16[2,64,128]{2,1,0:T(8,128)(2,1)S(1)}, bf16[2,64,128]{2,1,0:T(8,128)(2,1)S(1)}, u32[]{:S(2)}, u32[]{:S(2)}) collective-permute-start(bf16[2,64,128]{2,1,0:T(8,128)(2,1)S(1)} %get-tuple-element.167), channel_id=1, source_target_pairs={{1,0},{2,1},{3,2},{4,3},{5,4},{6,5},{7,6},{8,7},{9,8},{10,9},{11,1... | collective-permute-start | bytes 98312 | tf_op jit(solution)/shard_map/ppermute | solution.py:22
  349.0 21.5 %copy-start.3 = (f32[4,2,128,128]{3,2,1,0:T(8,128)S(1)}, f32[4,2,128,128]{3,2,1,0:T(8,128)}, u32[]{:S(2)}) copy-start(f32[4,2,128,128]{3,2,1,0:T(8,128)} %param.13) | copy-start | bytes 1572868
  372.4 210.4 %all-reduce.6.cloned.1.call-start = ((), (), s32[]{:S(2)}) async-start(), calls=%async_computation.6 | async-start | bytes 524288 | tf_op jit(solution)/shard_map/psum | solution.py:126
  437.1 394.8 %all-reduce.8.cloned.1.call-start = ((), (), s32[]{:S(2)}) async-start(), calls=%async_computation.7 | async-start | bytes 131072 | tf_op jit(solution)/shard_map/psum | solution.py:131
  582.8 275.5 %copy-start.5 = (f32[4,128,128]{2,1,0:T(8,128)S(1)}, f32[4,128,128]{2,1,0:T(8,128)}, u32[]{:S(2)}) copy-start(f32[4,128,128]{2,1,0:T(8,128)} %all-reduce.6.cloned.1.call-done) | copy-start | bytes 786436
  (10 other events, 22.0 us)
Sparse Core Ops, SparseCore 0:
  53.7 40.2 reduce-scatter.2
  97.1 74.2 all-gather.1
  335.2 34.3 reduce-scatter.4
  372.5 64.5 all-reduce.3
  440.4 142.3 all-reduce.5
  588.7 243.1 all-reduce.7
